TPU v7x, 32 devices: a whole 2x2x4 slice. The times are simulated.
32 devices in a mesh: dp: 4 (over z), span: 2 (over core), tensor: 4 (over y, x).
Axes of the slice: x: 2, y: 2, z: 4, core: 2. Of those that a mesh axis runs over, the one named last changes fastest.
Arguments:
- layer_input: bfloat16 [2, 16, 512, 768], P('span', 'dp', 'tensor'), may hold values from -6 to 6
- skip_tokens: bfloat16 [2, 16, 512, 768], P('span', 'dp', 'tensor'), may hold values from -6 to 6
- backbone_cotangent: bfloat16 [2, 16, 512, 768], P('span', 'dp', 'tensor'), may hold values from -6 to 6
- head_cotangent: bfloat16 [2, 16, 512, 768], P('span', 'dp', 'tensor'), may hold values from -6 to 6
- segment_lengths: int32 [2, 16, 4], P('span', 'dp'), may hold values from 1 to 174, 464 in all within a row
- pair_index: int32 [64], replicated, may hold values from 0 to 63, each once
- w_heads: bfloat16 [2, 3, 768, 768], P(None, None, None, 'tensor'), may hold values from -0.21875 to 0.21875
- heads_bias: bfloat16 [2, 2, 768], P(None, None, 'tensor'), may hold values from -1.75 to 1.75
- w_project: bfloat16 [2, 768, 768], P(None, 'tensor'), may hold values from -0.875 to 0.875
- project_bias: bfloat16 [2, 768], replicated, may hold values from -1.75 to 1.75
- norm_gain: bfloat16 [2, 2, 768], replicated, may hold values from 0.5 to 1.5
- norm_shift: bfloat16 [2, 2, 768], replicated, may hold values from -1.75 to 1.75
- w_expand: bfloat16 [2, 768, 3072], P(None, None, 'tensor'), may hold values from -0.21875 to 0.21875
- expand_bias: bfloat16 [2, 3072], P(None, 'tensor'), may hold values from -3 to 3
- w_shrink: bfloat16 [2, 3072, 768], P(None, 'tensor'), may hold values from -0.109375 to 0.109375
- shrink_bias: bfloat16 [2, 768], replicated, may hold values from -1.75 to 1.75
Outputs:
- backbone_out: bfloat16 [2, 16, 512, 768], P('span', 'dp', 'tensor')
- head_out: bfloat16 [2, 16, 512, 768], P('span', 'dp', 'tensor')
- span_loss: float32 [], replicated
- grad_input: bfloat16 [2, 16, 512, 768], P('span', 'dp', 'tensor')
- grad_skip: bfloat16 [2, 16, 512, 768], P('span', 'dp', 'tensor')
- grad_heads: float32 [2, 3, 768, 768], P(None, None, None, 'tensor')
- grad_heads_bias: float32 [2, 2, 768], P(None, None, 'tensor')
- grad_project: float32 [2, 768, 768], P(None, 'tensor')
- grad_project_bias: float32 [2, 768], replicated
- grad_gain: float32 [2, 2, 768], replicated
- grad_shift: float32 [2, 2, 768], replicated
- grad_expand: float32 [2, 768, 3072], P(None, None, 'tensor')
- grad_expand_bias: float32 [2, 3072], P(None, 'tensor')
- grad_shrink: float32 [2, 3072, 768], P(None, 'tensor')
- grad_shrink_bias: float32 [2, 768], replicated
Inputs may be any that keep to these rules, and one draw needn't show every extreme that they name: `segment_lengths`: each row holds 4 spans whose lengths add up to 464, the longest being 174; the rest of the row is padding. `pair_index`: each value occurs exactly once.
All inputs are finite; a program needn't handle non-finite values.
Results may differ from a plain program's by a relative error of at most 0.015.
The roundings to bfloat16 on the way count: a program that leaves them out, or rounds other values in their place, can miss the bound.
Values may be sent and summed in bfloat16 or wider, within the bound.
A program may use at most 192 MiB of HBM per device.

v0:
```python
import math
import jax
import jax.numpy as jnp
from jax import lax
from jax.sharding import PartitionSpec as P

HEAD_DIM = 64
EPSILON = 1e-12
LOSS_WEIGHT = 8.0
HIGHEST = lax.Precision.HIGHEST
MASKED = -1e30
BF = jnp.bfloat16
F32 = jnp.float32
BOTH = ("span", "tensor")


def mm(a, b, ca, cb):
    return lax.dot_general(a, b, (((ca,), (cb,)), ((), ())), preferred_element_type=F32)


def normal_parts(values):
    centred = values - jnp.mean(values, axis=-1, keepdims=True)
    spread = jnp.mean(centred * centred, axis=-1, keepdims=True)
    scale = lax.rsqrt(spread + EPSILON)
    return (centred * scale, scale)


def normal_back(upward, normed, scale, gain):
    weighted = upward * gain
    first = jnp.mean(weighted, axis=-1, keepdims=True)
    second = jnp.mean(weighted * normed, axis=-1, keepdims=True)
    return (weighted - first - normed * second) * scale


def split_heads(values):
    return values.reshape(values.shape[0], values.shape[1] // HEAD_DIM, HEAD_DIM)


def attend_forward(queries, keys, values, same):
    scores = (
        jnp.einsum(
            "qhd,khd->hqk", split_heads(queries), split_heads(keys), preferred_element_type=F32
        )
        * 0.125
    )
    scores = jnp.where(same[None], scores, MASKED)
    maximum = jnp.max(scores, axis=-1, keepdims=True)
    raised = jnp.exp(scores - maximum)
    total = jnp.sum(raised, axis=-1, keepdims=True)
    attention = (raised / total).astype(BF)
    mixture = jnp.einsum("hqk,khd->qhd", attention, split_heads(values), preferred_element_type=F32)
    return (mixture.reshape(queries.shape).astype(BF), maximum + jnp.log(total))


def attend_backward(queries, keys, values, same, upward, log_total):
    qh, kh, vh, uh = (split_heads(m) for m in (queries, keys, values, upward))
    scores = jnp.einsum("qhd,khd->hqk", qh, kh, preferred_element_type=F32) * 0.125
    scores = jnp.where(same[None], scores, MASKED)
    attention = jnp.exp(scores - log_total)
    grad_weights = jnp.einsum("qhd,khd->hqk", uh, vh, preferred_element_type=F32)
    inner = jnp.sum(attention * grad_weights, axis=-1, keepdims=True)
    grad_scores = (attention * (grad_weights - inner)).astype(BF)
    dq = jnp.einsum("hqk,khd->qhd", grad_scores, kh, preferred_element_type=F32) * 0.125
    dk = jnp.einsum("hqk,qhd->khd", grad_scores, qh, preferred_element_type=F32) * 0.125
    dv = jnp.einsum("hqk,qhd->khd", attention.astype(BF), uh, preferred_element_type=F32)
    return tuple((m.reshape(queries.shape).astype(BF) for m in (dq, dk, dv)))


def gelu_parts(hidden):
    phi = 0.5 * (1.0 + lax.erf(hidden * math.sqrt(0.5)))
    slope = phi + hidden * jnp.exp(-0.5 * hidden * hidden) * (1.0 / math.sqrt(2.0 * math.pi))
    return (hidden * phi, slope)


def layer_forward(x, same, attn_w, ffn_w, vec):
    wq, wk, wv, wp = attn_w
    we, ws = ffn_w
    xb = x.astype(BF)
    q = (mm(xb, wq, 1, 1) + vec["qb"]).astype(BF)
    k = mm(xb, wk, 1, 1).astype(BF)
    v = (mm(xb, wv, 1, 1) + vec["vb"]).astype(BF)
    o, lse = attend_forward(q, k, v, same)
    z1 = x + mm(o, wp, 1, 0) + vec["pb"]
    n1, r1 = normal_parts(z1)
    y = n1 * vec["g0"] + vec["s0"]
    yb = y.astype(BF)
    hid = jnp.einsum("qd,tdf->tqf", yb, we, preferred_element_type=F32) + vec["eb"][:, None, :]
    act, slope = gelu_parts(hid)
    act = act.astype(BF)
    z2 = y + jnp.einsum("tqf,tfd->qd", act, ws, preferred_element_type=F32) + vec["sb"]
    n2, r2 = normal_parts(z2)
    out = n2 * vec["g1"] + vec["s1"]
    return (out, (xb, q, k, v, o, lse, n1, r1, yb, act, slope.astype(BF), n2, r2))


def layer_backward(dout, same, attn_w, ffn_w, vec, kept):
    wq, wk, wv, wp = attn_w
    we, ws = ffn_w
    xb, q, k, v, o, lse, n1, r1, yb, act, slope, n2, r2 = kept
    dz2 = normal_back(dout, n2, r2, vec["g1"])
    dgain1 = jnp.sum(dout * n2, axis=0)
    dshift1 = jnp.sum(dout, axis=0)
    dsb = jnp.sum(dz2, axis=0)
    dzb = dz2.astype(BF)
    dws = jnp.einsum("tqf,qd->tfd", act, dzb, preferred_element_type=F32).astype(BF)
    dact = jnp.einsum("qd,tfd->tqf", dzb, ws, preferred_element_type=F32)
    dhid = dact * slope.astype(F32)
    deb = jnp.sum(dhid, axis=1)
    dhb = dhid.astype(BF)
    dwe = jnp.einsum("qd,tqf->tdf", yb, dhb, preferred_element_type=F32).astype(BF)
    dy = dz2 + jnp.einsum("tqf,tdf->qd", dhb, we, preferred_element_type=F32)
    dz1 = normal_back(dy, n1, r1, vec["g0"])
    dgain0 = jnp.sum(dy * n1, axis=0)
    dshift0 = jnp.sum(dy, axis=0)
    dpb = jnp.sum(dz1, axis=0)
    da = dz1.astype(BF)
    dwp = mm(o, da, 0, 0).astype(BF)
    do = mm(da, wp, 1, 1).astype(BF)
    dq, dk, dv = attend_backward(q, k, v, same, do, lse)
    dwq = mm(dq, xb, 0, 0).astype(BF)
    dwk = mm(dk, xb, 0, 0).astype(BF)
    dwv = mm(dv, xb, 0, 0).astype(BF)
    dqb = jnp.sum(dq.astype(F32), axis=0)
    dvb = jnp.sum(dv.astype(F32), axis=0)
    dx = dz1 + mm(dq, wq, 1, 0) + mm(dk, wk, 1, 0) + mm(dv, wv, 1, 0)
    small = {
        "qb": dqb,
        "vb": dvb,
        "pb": dpb,
        "g0": dgain0,
        "g1": dgain1,
        "s0": dshift0,
        "s1": dshift1,
        "sb": dsb,
        "eb": deb.reshape(-1),
    }
    return (dx, (dwq, dwk, dwv, dwp), (dwe, dws), small)


SMALL = ("qb", "vb", "pb", "g0", "g1", "s0", "s1", "sb", "eb")


def to_rows(values):
    return lax.all_to_all(values, "tensor", split_axis=0, concat_axis=1, tiled=True)[0]


def to_places(values):
    return lax.all_to_all(values[None], "tensor", split_axis=1, concat_axis=0, tiled=True)


def shards(
    layer_input,
    skip_tokens,
    backbone_cotangent,
    head_cotangent,
    segment_lengths,
    pair_index,
    w_heads,
    heads_bias,
    w_project,
    project_bias,
    norm_gain,
    norm_shift,
    w_expand,
    expand_bias,
    w_shrink,
    shrink_bias,
):
    side = lax.axis_index("span")
    mine = lax.axis_index("tensor")
    tensor_count = lax.axis_size("tensor")
    width = layer_input.shape[-1]
    head_cols = w_heads.shape[-1]
    ff_cols = w_expand.shape[-1]

    def gather_attn(l):
        heads = jnp.swapaxes(w_heads[l], 1, 2)
        zero = jnp.stack([heads[0], heads[1]])
        one = jnp.stack([heads[2], w_project[l]])
        got = lax.all_gather(jnp.where(side == 0, zero, one), BOTH, axis=0, tiled=False)
        got = got.reshape(2, tensor_count, 2, head_cols, width)
        return tuple(
            (
                got[i, :, j].reshape(tensor_count * head_cols, width)
                for i in range(2)
                for j in range(2)
            )
        )

    def gather_ffn(l):
        got = lax.all_gather(
            jnp.where(side == 0, w_expand[l], w_shrink[l]), BOTH, axis=0, tiled=False
        )
        got = got.reshape(2, tensor_count, width, ff_cols)
        return (got[0], got[1])

    small_in = jnp.concatenate([heads_bias.reshape(-1), expand_bias.reshape(-1)])
    small_got = lax.all_gather(small_in, "tensor", axis=0, tiled=False).astype(F32)
    hb_all = jnp.transpose(
        small_got[:, : 4 * head_cols].reshape(tensor_count, 2, 2, head_cols), (1, 2, 0, 3)
    )
    hb_all = hb_all.reshape(2, 2, tensor_count * head_cols)
    eb_all = jnp.transpose(
        small_got[:, 4 * head_cols :].reshape(tensor_count, 2, ff_cols), (1, 0, 2)
    )

    def vectors(l):
        return {
            "qb": hb_all[l, 0],
            "vb": hb_all[l, 1],
            "pb": project_bias[l].astype(F32),
            "g0": norm_gain[l, 0].astype(F32),
            "g1": norm_gain[l, 1].astype(F32),
            "s0": norm_shift[l, 0].astype(F32),
            "s1": norm_shift[l, 1].astype(F32),
            "sb": shrink_bias[l].astype(F32),
            "eb": eb_all[l],
        }

    attn_w0 = gather_attn(0)
    ffn_w0 = gather_ffn(0)
    attn_w1 = gather_attn(1)
    ffn_w1 = gather_ffn(1)
    x = to_rows(layer_input[0])
    skip = to_rows(skip_tokens[0])
    backbone_cot = to_rows(backbone_cotangent[0])
    head_cot = to_rows(head_cotangent[0])
    tokens = x.shape[0]
    lengths = lax.dynamic_index_in_dim(segment_lengths[0], mine, 0, keepdims=False)
    span_count = lengths.shape[0]
    starts = jnp.cumsum(lengths) - lengths
    row_length = jnp.sum(lengths)
    places = jnp.arange(tokens, dtype=jnp.int32)
    counted = jnp.sum((places[:, None] >= starts[None, :]).astype(jnp.int32), axis=-1) - 1
    segment = jnp.where(places < row_length, counted, span_count)
    same = segment[:, None] == segment[None, :]
    valid = (places < row_length).astype(F32)[:, None]
    picker = (starts[:, None] == places[None, :]).astype(F32)
    first = jnp.sum(picker, axis=0)[:, None] > 0
    vec0, vec1 = (vectors(0), vectors(1))
    backbone, kept0 = layer_forward(x.astype(F32), same, attn_w0, ffn_w0, vec0)
    cls = mm(picker.astype(BF), backbone.astype(BF), 1, 0).astype(BF)
    anchors = lax.all_gather(cls, ("dp", "span", "tensor"), axis=0, tiled=False)
    dp_count = lax.axis_size("dp")
    pair_count = lax.axis_size("span")
    anchors = anchors.reshape(dp_count, pair_count, tensor_count * span_count, width)
    anchors = jnp.swapaxes(anchors, 0, 1).reshape(
        pair_count, dp_count * tensor_count * span_count, width
    )
    head_in = jnp.where(first, backbone, skip.astype(F32))
    head, kept1 = layer_forward(head_in, same, attn_w1, ffn_w1, vec1)
    vector_count = anchors.shape[1]
    root = math.sqrt(width)
    logits = mm(anchors[0], anchors[1], 1, 1) / root
    columns = jnp.arange(vector_count, dtype=jnp.int32)
    target = (pair_index[:, None] == columns[None, :]).astype(F32)
    lse_rows = jax.nn.logsumexp(logits, axis=1)
    lse_cols = jax.nn.logsumexp(logits, axis=0)
    dlogits = LOSS_WEIGHT * (
        jnp.exp(logits - lse_rows[:, None]) + jnp.exp(logits - lse_cols[None, :]) - 2.0 * target
    )
    span_loss = (jnp.sum(lse_rows) + jnp.sum(lse_cols) - 2.0 * jnp.sum(target * logits)) / (
        2 * vector_count
    )
    own = (lax.axis_index("dp") * tensor_count + mine) * span_count
    wanted = jnp.where(side == 0, dlogits, dlogits.T)
    wanted = lax.dynamic_slice(wanted, (own, 0), (span_count, vector_count))
    other = lax.dynamic_index_in_dim(anchors, 1 - side, 0, keepdims=False).astype(F32)
    dcls = jnp.dot(wanted, other, precision=HIGHEST) / root
    du, dattn1, dffn1, small1 = layer_backward(
        head_cot.astype(F32) * valid, same, attn_w1, ffn_w1, vec1, kept1
    )
    grad_skip = jnp.where(first, 0.0, du).astype(BF)
    seed = backbone_cot.astype(F32) * valid + jnp.where(first, du, 0.0)
    seed = seed + jnp.dot(picker.T, dcls, precision=HIGHEST)
    dx, dattn0, dffn0, small0 = layer_backward(seed, same, attn_w0, ffn_w0, vec0, kept0)

    def reduce_attn(grads):
        packed = jnp.stack([g.reshape(tensor_count, head_cols, width) for g in grads])
        packed = packed.reshape(2, 2, tensor_count, head_cols, width)
        packed = jnp.swapaxes(packed, 1, 2).reshape(2 * tensor_count, 2, head_cols, width)
        part = lax.psum_scatter(packed, BOTH, scatter_dimension=0, tiled=False)
        part = lax.psum(part, "dp")
        got = lax.all_gather(part, "span", axis=0, tiled=False).astype(F32)
        heads = jnp.stack([got[0, 0], got[0, 1], got[1, 0]])
        return (jnp.swapaxes(heads, 1, 2), got[1, 1])

    def reduce_ffn(grads):
        packed = jnp.stack(grads).reshape(2 * tensor_count, width, ff_cols)
        part = lax.psum_scatter(packed, BOTH, scatter_dimension=0, tiled=False)
        part = lax.psum(part, "dp")
        got = lax.all_gather(part, "span", axis=0, tiled=False).astype(F32)
        return (got[0], got[1])

    ge1, gs1 = reduce_ffn(dffn1)
    gh1, gp1 = reduce_attn(dattn1)
    ge0, gs0 = reduce_ffn(dffn0)
    gh0, gp0 = reduce_attn(dattn0)
    flat = jnp.concatenate([small[k] for small in (small0, small1) for k in SMALL])
    flat = lax.psum(flat, ("dp", "span", "tensor"))
    sizes = [small0[k].shape[0] for k in SMALL] * 2
    cuts = []
    at = 0
    for size in sizes:
        cuts.append(flat[at : at + size])
        at += size
    s0 = dict(zip(SMALL, cuts[: len(SMALL)]))
    s1 = dict(zip(SMALL, cuts[len(SMALL) :]))

    def local(values, size):
        return lax.dynamic_slice(values, (mine * size,), (size,))

    hb = jnp.stack(
        [jnp.stack([local(s["qb"], head_cols), local(s["vb"], head_cols)]) for s in (s0, s1)]
    )
    eb = jnp.stack([local(s["eb"], ff_cols) for s in (s0, s1)])
    return (
        to_places((backbone * valid).astype(BF))[None],
        to_places((head * valid).astype(BF))[None],
        span_loss,
        to_places(dx.astype(BF))[None],
        to_places(grad_skip)[None],
        jnp.stack([gh0, gh1]),
        hb,
        jnp.stack([gp0, gp1]),
        jnp.stack([s0["pb"], s1["pb"]]),
        jnp.stack([jnp.stack([s["g0"], s["g1"]]) for s in (s0, s1)]),
        jnp.stack([jnp.stack([s["s0"], s["s1"]]) for s in (s0, s1)]),
        jnp.stack([ge0, ge1]),
        eb,
        jnp.stack([gs0, gs1]),
        jnp.stack([s0["sb"], s1["sb"]]),
    )


def solution(mesh):
    rows = P("span", "dp", "tensor", None)
    in_specs = (
        rows,
        rows,
        rows,
        rows,
        P("span", "dp", None),
        P(),
        P(None, None, None, "tensor"),
        P(None, None, "tensor"),
        P(None, "tensor", None),
        P(),
        P(),
        P(),
        P(None, None, "tensor"),
        P(None, "tensor"),
        P(None, "tensor", None),
        P(),
    )
    out_specs = (
        rows,
        rows,
        P(),
        rows,
        rows,
        P(None, None, None, "tensor"),
        P(None, None, "tensor"),
        P(None, "tensor", None),
        P(),
        P(),
        P(),
        P(None, None, "tensor"),
        P(None, "tensor"),
        P(None, "tensor", None),
        P(),
    )
    return jax.shard_map(shards, mesh=mesh, in_specs=in_specs, out_specs=out_specs, check_vma=False)
```

profile of v0, /device:TPU:0, one launch (start us, length us, event | category | flops | bytes accessed | tf_op | source)
XLA Modules:
  0.0 985.8 jit_solution(689958023518793474)
XLA Ops:
  25.8 16.1 %all-gather.4 = bf16[4,1,2304]{2,1,0:T(2,128)(2,1)S(1)} all-gather(bf16[1,1,2304]{2,1,0:T(2,128)(2,1)S(1)} %reshape.546), channel_id=3, replica_groups=mesh['dp'=4,'span'=2,'tensor'=4] {'tensor'}, dimensions={0}, use_global_device_ids=true | all-gather | bytes 23040 | tf_op jit(solution)/shard_map/all_gather | solution.py:198
  49.3 20.0 %all-gather.27.cloned.1.call-done = bf16[16,192,768]{2,1,0:T(8,128)(2,1)} async-done(((bf16[2,192,768]{2,1,0:T(8,128)(2,1)}), bf16[16,192,768]{2,1,0:T(8,128)(2,1)}) %all-gather.27.cloned.1.call-update) | async-done | bytes 4718608 | tf_op jit(solution)/shard_map/all_gather | solution.py:180
  96.6 21.1 %all-gather.29.cloned.1.call-done = bf16[16,192,768]{2,1,0:T(8,128)(2,1)} async-done(((bf16[2,192,768]{2,1,0:T(8,128)(2,1)}), bf16[16,192,768]{2,1,0:T(8,128)(2,1)}) %all-gather.29.cloned.1.call-update) | async-done | bytes 4718608 | tf_op jit(solution)/shard_map/all_gather | solution.py:180
  122.4 56.6 %all-gather.15.cloned.1.call-done = bf16[8,768,768]{2,1,0:T(8,128)(2,1)} async-done(((bf16[1,768,768]{2,1,0:T(8,128)(2,1)}), bf16[8,768,768]{2,1,0:T(8,128)(2,1)}) %all-gather.15.cloned.1.call-update) | async-done | bytes 9437200 | tf_op jit(solution)/shard_map/all_gather | solution.py:191
  189.9 69.3 %all-gather.5 = bf16[32,4,768]{2,1,0:T(4,128)(2,1)S(1)} all-gather(bf16[1,4,768]{2,1,0:T(4,128)(2,1)S(1)} %fusion.74), channel_id=5, replica_groups=mesh['dp'=4,'span'=2,'tensor'=4] {'dp','span','tensor'}, dimensions={0}, use_global_device_ids=true | all-gather | bytes 202752 | tf_op jit(solution)/shard_map/all_gather | solution.py:243
  313.2 9.8 multiply_reduce_fusion.3
  331.5 9.6 convert_reduce_fusion
  341.1 9.7 multiply_reduce_fusion.1
  386.9 8.0 fusion.38
  404.0 8.3 convert_reduce_fusion.2
  414.0 11.2 %multiply_reduce_fusion = (f32[12,512]{1,0:T(8,128)S(1)}, f32[12,512,512]{1,2,0:T(8,128)}) fusion(f32[12,512]{1,0:T(8,128)S(1)} %copy-done.66, f32[12,512,512]{1,2,0:T(8,128)} %copy-done, pred[512,512]{0,1:T(8,128)(4,1)S(1)} %broadcast_compare_fusion, bf16[512,12,64]{0,2,1:T(8,128)(2,1)S(1)} %bitcast.409, bf16[512,12,64]{0,2,1:T(8,128)(2,1)S(1)} %bitcast.439), kind=kOutput, calls=%fused_computation.1 | convolution fusion | flops 418375680 | bytes 27049984 | tf_op jit(solution)/shard_map/qhd,khd->hqk/dot_general | solution.py:60
  443.1 7.4 convert_bitcast_fusion
  450.5 8.4 convert_bitcast_fusion.1
  458.9 8.4 pad_maximum_fusion.1
  467.3 12.7 %copy.209 = bf16[8,768,768]{2,1,0:T(8,128)(2,1)} copy(bf16[8,768,768]{1,2,0:T(8,128)(2,1)} %bitcast.378) | data formatting | bytes 18874368 | tf_op jit(solution)/shard_map/reshape | solution.py:289
  487.9 7.7 convert_bitcast_fusion.3
  495.6 8.3 pad_maximum_fusion
  503.9 13.5 %copy.205 = bf16[8,768,768]{2,1,0:T(8,128)(2,1)} copy(bf16[8,768,768]{1,2,0:T(8,128)(2,1)} %bitcast.379) | data formatting | bytes 18874368 | tf_op jit(solution)/shard_map/reshape | solution.py:289
  517.5 58.3 %reduce-scatter.11.cloned.1.call-done = bf16[1,768,768]{2,1,0:T(8,128)(2,1)} async-done(((bf16[8,768,768]{2,1,0:T(8,128)(2,1)}), bf16[1,768,768]{2,1,0:T(8,128)(2,1)}) %reduce-scatter.11.cloned.1.call-update) | async-done | bytes 1179664 | tf_op jit(solution)/shard_map/reduce_scatter | solution.py:290
  575.7 80.3 %reduce-scatter.9.cloned.1.call-done = bf16[1,768,768]{2,1,0:T(8,128)(2,1)} async-done(((bf16[8,768,768]{2,1,0:T(8,128)(2,1)}), bf16[1,768,768]{2,1,0:T(8,128)(2,1)}) %reduce-scatter.9.cloned.1.call-update) | async-done | bytes 1179664 | tf_op jit(solution)/shard_map/reduce_scatter | solution.py:290
  658.1 134.5 %all-reduce.6.cloned.1.call-done = (bf16[1,2,192,768]{3,2,1,0:T(8,128)(2,1)}, bf16[1,2,192,768]{3,2,1,0:T(8,128)(2,1)}, bf16[1,768,768]{2,1,0:T(8,128)(2,1)}, bf16[1,768,768]{2,1,0:T(8,128)(2,1)}) async-done(((bf16[1,2,192,768]{3,2,1,0:T(8,128)(2,1)}, bf16[1,2,192,768]{3,2,1,0:T(8,128)(2,1)}, bf16[1,768,768]{2,1,0:T(8,128)(2,1)}, bf16[1,768,768]{2,1,0:T(8,128)(2,1)}), (bf16[1,2,192,768]{3,2,1,0:T(8,128)(2,1)}, ...) | async-done | bytes 3538960 | tf_op jit(solution)/shard_map/psum | solution.py:283
  847.2 71.1 %all-reduce.4.cloned.1.call-done = f32[18432]{0:T(1024)} async-done(((f32[18432]{0:T(1024)}), f32[18432]{0:T(1024)}) %all-reduce.4.cloned.1.call-update) | async-done | bytes 73744 | tf_op jit(solution)/shard_map/psum | solution.py:300
  925.2 10.3 %all-to-all-done.7 = bf16[4,2,49152]{2,1,0:T(2,128)(2,1)S(1)} async-done(((bf16[4,2,49152]{2,1,0:T(2,128)(2,1)}), bf16[4,2,49152]{2,1,0:T(2,128)(2,1)S(1)}, u32[]{:S(2)}, u32[]{:S(2)}) %all-to-all-start.7) | async-done | bytes 786464 | tf_op jit(solution)/shard_map/all_to_all | solution.py:148
  962.3 8.0 all-gather.25.cloned.1.call-done
  (510 shorter events, 298.0 us)
Async XLA Ops:
  7.2 62.2 %all-gather.27.cloned.1.call-start = ((), (), s32[]{:S(2)}) async-start(), calls=%async_computation.23 | async-start | bytes 5308416 | tf_op jit(solution)/shard_map/all_gather | solution.py:180
  10.8 106.9 %all-gather.29.cloned.1.call-start = ((), (), s32[]{:S(2)}) async-start(), calls=%async_computation.24 | async-start | bytes 5308416 | tf_op jit(solution)/shard_map/all_gather | solution.py:180
  11.8 167.1 %all-gather.15.cloned.1.call-start = ((), (), s32[]{:S(2)}) async-start(), calls=%async_computation.12 | async-start | bytes 10616832 | tf_op jit(solution)/shard_map/all_gather | solution.py:191
  16.1 28.2 %all-to-all-start.5 = ((bf16[4,128,768]{2,1,0:T(8,128)(2,1)}), bf16[4,128,768]{2,1,0:T(8,128)(2,1)S(1)}, u32[]{:S(2)}, u32[]{:S(2)}) async-start(bf16[4,128,768]{2,1,0:T(8,128)(2,1)} %bitcast.446), calls=%async_computation.5 | async-start | bytes 1572864 | tf_op jit(solution)/shard_map/all_to_all | solution.py:144
  21.4 273.8 %all-gather.17.cloned.1.call-start = ((), (), s32[]{:S(2)}) async-start(), calls=%async_computation.13 | async-start | bytes 10616832 | tf_op jit(solution)/shard_map/all_gather | solution.py:191
  22.8 166.7 %copy-start.88 = (s32[4]{0:T(128)}, s32[4]{0:T(128)S(1)}, u32[]{:S(2)}) copy-start(s32[4]{0:T(128)S(1)} %bitcast_subtract_fusion) | copy-start | bytes 52
  23.7 267.7 %copy-start.94 = (pred[512]{0:T(512)(128)(4,1)}, pred[512]{0:T(512)(128)(4,1)S(1)}, u32[]{:S(2)}) copy-start(pred[512]{0:T(512)(128)(4,1)S(1)} %broadcast_compare_fusion.1) | copy-start | bytes 1540
  44.3 29.3 %all-to-all-start = ((bf16[4,128,768]{2,1,0:T(8,128)(2,1)}), bf16[4,128,768]{2,1,0:T(8,128)(2,1)S(1)}, u32[]{:S(2)}, u32[]{:S(2)}) async-start(bf16[4,128,768]{2,1,0:T(8,128)(2,1)} %bitcast), calls=%async_computation | async-start | bytes 1572864 | tf_op jit(solution)/shard_map/all_to_all | solution.py:144
  73.5 186.5 %all-to-all-start.2 = ((bf16[4,128,768]{2,1,0:T(8,128)(2,1)}), bf16[4,128,768]{2,1,0:T(8,128)(2,1)}, u32[]{:S(2)}, u32[]{:S(2)}) async-start(bf16[4,128,768]{2,1,0:T(8,128)(2,1)} %bitcast.29), calls=%async_computation.2 | async-start | bytes 1572864 | tf_op jit(solution)/shard_map/all_to_all | solution.py:144
  260.0 122.0 %all-to-all-start.4 = ((bf16[4,128,768]{2,1,0:T(8,128)(2,1)}), bf16[4,128,768]{2,1,0:T(8,128)(2,1)}, u32[]{:S(2)}, u32[]{:S(2)}) async-start(bf16[4,128,768]{2,1,0:T(8,128)(2,1)} %bitcast.54), calls=%async_computation.4 | async-start | bytes 1572864 | tf_op jit(solution)/shard_map/all_to_all | solution.py:144
  264.3 253.2 %reduce-scatter.7.cloned.1.call-start = ((), (), s32[]{:S(2)}) async-start(), calls=%async_computation.16 | async-start | bytes 5308416 | tf_op jit(solution)/shard_map/reduce_scatter | solution.py:282
  375.5 142.0 %reduce-scatter.5.cloned.1.call-start = ((), (), s32[]{:S(2)}) async-start(), calls=%async_computation.14 | async-start | bytes 5308416 | tf_op jit(solution)/shard_map/reduce_scatter | solution.py:282
  442.7 133.0 %reduce-scatter.11.cloned.1.call-start = ((), (), s32[]{:S(2)}) async-start(), calls=%async_computation.21 | async-start | bytes 10616832 | tf_op jit(solution)/shard_map/reduce_scatter | solution.py:290
  480.0 176.1 %reduce-scatter.9.cloned.1.call-start = ((), (), s32[]{:S(2)}) async-start(), calls=%async_computation.19 | async-start | bytes 10616832 | tf_op jit(solution)/shard_map/reduce_scatter | solution.py:290
  517.4 275.2 %all-reduce.6.cloned.1.call-start = ((), (), s32[]{:S(2)}) async-start(), calls=%async_computation.25 | async-start | bytes 7077888 | tf_op jit(solution)/shard_map/psum | solution.py:283
  656.2 262.2 %all-reduce.4.cloned.1.call-start = ((), (), s32[]{:S(2)}) async-start(), calls=%async_computation.18 | async-start | bytes 147456 | tf_op jit(solution)/shard_map/psum | solution.py:300
  658.0 294.1 %all-gather.19.cloned.1.call-start = ((), (), s32[]{:S(2)}) async-start(), calls=%async_computation.15 | async-start | bytes 1769472 | tf_op jit(solution)/shard_map/all_gather | solution.py:284
  792.6 161.1 %all-gather.21.cloned.1.call-start = ((), (), s32[]{:S(2)}) async-start(), calls=%async_computation.17 | async-start | bytes 1769472 | tf_op jit(solution)/shard_map/all_gather | solution.py:284
  804.3 19.2 %all-to-all-start.1 = ((bf16[4,2,49152]{2,1,0:T(2,128)(2,1)}), bf16[4,2,49152]{2,1,0:T(2,128)(2,1)}, u32[]{:S(2)}, u32[]{:S(2)}) async-start(bf16[4,2,49152]{2,1,0:T(2,128)(2,1)} %reshape.577), calls=%async_computation.1 | async-start | bytes 1572864 | tf_op jit(solution)/shard_map/all_to_all | solution.py:148
  808.5 150.4 %all-gather.23.cloned.1.call-start = ((), (), s32[]{:S(2)}) async-start(), calls=%async_computation.20 | async-start | bytes 3538944 | tf_op jit(solution)/shard_map/all_gather | solution.py:292
  823.6 96.4 %all-to-all-start.3 = ((bf16[4,2,49152]{2,1,0:T(2,128)(2,1)}), bf16[4,2,49152]{2,1,0:T(2,128)(2,1)}, u32[]{:S(2)}, u32[]{:S(2)}) async-start(bf16[4,2,49152]{2,1,0:T(2,128)(2,1)} %reshape.579), calls=%async_computation.3 | async-start | bytes 1572864 | tf_op jit(solution)/shard_map/all_to_all | solution.py:148
  920.0 15.5 %all-to-all-start.7 = ((bf16[4,2,49152]{2,1,0:T(2,128)(2,1)}), bf16[4,2,49152]{2,1,0:T(2,128)(2,1)S(1)}, u32[]{:S(2)}, u32[]{:S(2)}) async-start(bf16[4,2,49152]{2,1,0:T(2,128)(2,1)} %reshape.583), calls=%async_computation.7 | async-start | bytes 1572864 | tf_op jit(solution)/shard_map/all_to_all | solution.py:148
  923.5 46.8 %all-gather.25.cloned.1.call-start = ((), (), s32[]{:S(2)}) async-start(), calls=%async_computation.22 | async-start | bytes 3538944 | tf_op jit(solution)/shard_map/all_gather | solution.py:292
  935.5 14.9 %all-to-all-start.6 = ((bf16[4,2,49152]{2,1,0:T(2,128)(2,1)}), bf16[4,2,49152]{2,1,0:T(2,128)(2,1)S(1)}, u32[]{:S(2)}, u32[]{:S(2)}) async-start(bf16[4,2,49152]{2,1,0:T(2,128)(2,1)} %reshape.581), calls=%async_computation.6 | async-start | bytes 1572864 | tf_op jit(solution)/shard_map/all_to_all | solution.py:148
  (114 other events, 1011.1 us)
Sparse Core Ops, SparseCore 0:
  11.0 58.3 all-gather.26
  71.8 45.9 all-gather.28
  120.2 58.6 all-gather.14
  181.2 60.4 all-gather.16
  375.6 52.3 reduce-scatter.6
  442.8 52.5 reduce-scatter.4
  498.9 76.8 reduce-scatter.10
  579.2 76.8 reduce-scatter.8
  658.7 133.8 all-reduce.5
  798.6 119.6 all-reduce.3
  919.9 11.2 all-gather.18
  932.6 10.3 all-gather.20
  944.6 12.1 all-gather.22
  958.1 12.1 all-gather.24
where the time goes:
time: 992 us; the launch traced here: 986 us
  waiting for transfers between devices  462 us (47%)
  matrix products  180 us (18%)
  local copies, waits for them, and re-layouts  102 us (10%)
  other arithmetic  102 us (10%)
  blocking collectives  85.4 us (9%)
  starting transfers between devices  34.9 us (4%)
  between operations  19.5 us (2%)
    reduce_scatter x2, waiting for transfers between devices, reduce_ffn(): part = lax.psum_scatter(packed, BOTH, scatter_dimension=0, tiled=False)  139 us
    psum x1, waiting for transfers between devices, reduce_attn(): part = lax.psum(part, 'dp')  135 us
    psum x1, waiting for transfers between devices, shards(): flat = lax.psum(flat, ('dp', 'span', 'tensor'))  71.1 us
    all_gather x1, blocking collectives, shards(): anchors = lax.all_gather(cls, ('dp', 'span', 'tensor'), axis=0, tiled=False)  69.3 us
    all_gather x2, waiting for transfers between devices, gather_ffn(): lax.all_gather(jnp.where(side == 0, w_expand[l], w_shrink[l]), BOTH, axis...  56.6 us
    dot_general x26, matrix products, mm(): lax.dot_general(a, b, (((ca,), (cb,)), ((), ())), preferred_element_type=...  43.4 us
    all_gather x2, waiting for transfers between devices, gather_attn(): lax.all_gather(jnp.where(side == 0, zero, one), BOTH, axis=0, tiled=False)  41.2 us
    unnamed x265, local copies, waits for them, and re-layouts  32.2 us
  transfers between devices with their start and end apart: 22, of which 10 were waited for; matrix products, arithmetic and copies ran while one was open for 36% of the time, Pallas kernels for 0%

commit v1 on v0

--- a/solution.py
+++ b/solution.py
@@ -12,6 +12,11 @@
 BF = jnp.bfloat16
 F32 = jnp.float32
 BOTH = ("span", "tensor")
+
+
+def link_counts(load):
+    d_next = jnp.sum(lax.all_gather(load, ("dp", "span", "tensor")), axis=0)
+    return d_next
 
 
 def mm(a, b, ca, cb):
@@ -297,7 +302,7 @@
     ge0, gs0 = reduce_ffn(dffn0)
     gh0, gp0 = reduce_attn(dattn0)
     flat = jnp.concatenate([small[k] for small in (small0, small1) for k in SMALL])
-    flat = lax.psum(flat, ("dp", "span", "tensor"))
+    flat = link_counts(flat)
     sizes = [small0[k].shape[0] for k in SMALL] * 2
     cuts = []
     at = 0

time: 992 us -> 922 us (0.929)
  waiting for transfers between devices: 462 us -> 386 us
    psum x1 -> x0, waiting for transfers between devices: 71.1 us -> none  [shards(): flat = lax.psum(flat, ('dp', 'span', 'tensor'))]
    all_to_all x4, waiting for transfers between devices: 10.5 us -> 0.36 us  [to_places(): lax.all_to_all(values[None], 'tensor', split_axis=1, concat_axis=0, tiled...]
    unnamed x265 -> x255, local copies, waits for them, and re-layouts: 32.2 us -> 31 us
  transfers between devices with their start and end apart: 22 -> 22, of which waited for: 10 -> 9; matrix products, arithmetic and copies ran while one was open for 36% -> 40% of each run, Pallas kernels for 0% -> 0%
where the time goes in v1:
time: 922 us; the launch traced here: 916 us
  waiting for transfers between devices  386 us (42%)
  matrix products  184 us (20%)
  other arithmetic  103 us (11%)
  local copies, waits for them, and re-layouts  101 us (11%)
  blocking collectives  85.4 us (9%)
  starting transfers between devices  36.7 us (4%)
  between operations  19.6 us (2%)
    reduce_scatter x2, waiting for transfers between devices, reduce_ffn(): part = lax.psum_scatter(packed, BOTH, scatter_dimension=0, tiled=False)  139 us
    psum x1, waiting for transfers between devices, reduce_attn(): part = lax.psum(part, 'dp')  134 us
    all_gather x1, blocking collectives, shards(): anchors = lax.all_gather(cls, ('dp', 'span', 'tensor'), axis=0, tiled=False)  69.3 us
    all_gather x2, waiting for transfers between devices, gather_ffn(): lax.all_gather(jnp.where(side == 0, w_expand[l], w_shrink[l]), BOTH, axis...  56.6 us
    dot_general x26, matrix products, mm(): lax.dot_general(a, b, (((ca,), (cb,)), ((), ())), preferred_element_type=...  47.8 us
    all_gather x2, waiting for transfers between devices, gather_attn(): lax.all_gather(jnp.where(side == 0, zero, one), BOTH, axis=0, tiled=False)  41.1 us
    unnamed x255, local copies, waits for them, and re-layouts  31 us
    reshape x2, local copies, waits for them, and re-layouts, reduce_ffn(): packed = jnp.stack(grads).reshape(2 * tensor_count, width, ff_cols)  26.1 us
  transfers between devices with their start and end apart: 22, of which 9 were waited for; matrix products, arithmetic and copies ran while one was open for 40% of the time, Pallas kernels for 0%

profile of v1, /device:TPU:0, one launch (start us, length us, event | category | flops | bytes accessed | tf_op | source)
XLA Modules:
  0.0 916.4 jit_solution(13287772961196696378)
XLA Ops:
  25.8 16.1 %all-gather.5 = bf16[4,1,2304]{2,1,0:T(2,128)(2,1)S(1)} all-gather(bf16[1,1,2304]{2,1,0:T(2,128)(2,1)S(1)} %reshape.547), channel_id=3, replica_groups=mesh['dp'=4,'span'=2,'tensor'=4] {'tensor'}, dimensions={0}, use_global_device_ids=true | all-gather | bytes 23040 | tf_op jit(solution)/shard_map/all_gather | solution.py:203
  49.3 20.0 %all-gather.29.cloned.1.call-done = bf16[16,192,768]{2,1,0:T(8,128)(2,1)} async-done(((bf16[2,192,768]{2,1,0:T(8,128)(2,1)}), bf16[16,192,768]{2,1,0:T(8,128)(2,1)}) %all-gather.29.cloned.1.call-update) | async-done | bytes 4718608 | tf_op jit(solution)/shard_map/all_gather | solution.py:185
  96.6 21.0 %all-gather.31.cloned.1.call-done = bf16[16,192,768]{2,1,0:T(8,128)(2,1)} async-done(((bf16[2,192,768]{2,1,0:T(8,128)(2,1)}), bf16[16,192,768]{2,1,0:T(8,128)(2,1)}) %all-gather.31.cloned.1.call-update) | async-done | bytes 4718608 | tf_op jit(solution)/shard_map/all_gather | solution.py:185
  122.3 56.6 %all-gather.17.cloned.1.call-done = bf16[8,768,768]{2,1,0:T(8,128)(2,1)} async-done(((bf16[1,768,768]{2,1,0:T(8,128)(2,1)}), bf16[8,768,768]{2,1,0:T(8,128)(2,1)}) %all-gather.17.cloned.1.call-update) | async-done | bytes 9437200 | tf_op jit(solution)/shard_map/all_gather | solution.py:196
  178.8 7.2 fusion.25
  189.6 69.3 %all-gather.6 = bf16[32,4,768]{2,1,0:T(4,128)(2,1)S(1)} all-gather(bf16[1,4,768]{2,1,0:T(4,128)(2,1)S(1)} %fusion.74), channel_id=5, replica_groups=mesh['dp'=4,'span'=2,'tensor'=4] {'dp','span','tensor'}, dimensions={0}, use_global_device_ids=true | all-gather | bytes 202752 | tf_op jit(solution)/shard_map/all_gather | solution.py:248
  312.9 9.8 %multiply_reduce_fusion.3 = (f32[768]{0:T(1024)}, f32[512]{0:T(512)S(1)}, f32[512]{0:T(512)S(1)}, f32[768]{0:T(1024)}, f32[512,768]{1,0:T(8,128)S(1)}) fusion(f32[512,768]{1,0:T(8,128)S(1)} %get-tuple-element.135, f32[512]{0:T(512)S(1)} %add_rsqrt_fusion.1, f32[512]{0:T(512)S(1)} %broadcast_multiply_fusion.8, f32[768]{0:T(1024)S(1)} %get-tuple-element.42, ...), kind=kOutput, calls=%fused_computation.91 | convolution fusion | flops 2424567296 | bytes 18891776 | tf_op jit(solution)/shard_map/tqf,tdf->qd/dot_general | solution.py:116
  331.2 9.6 %convert_reduce_fusion = (f32[12,64]{1,0:T(8,128)}, bf16[12,64,512]{2,1,0:T(8,128)(2,1)}) fusion(bf16[512,12,64]{0,2,1:T(8,128)(2,1)} %bitcast.410, f32[12,512]{1,0:T(8,128)S(1)} %log_add_fusion.1, f32[12,512,512]{1,2,0:T(8,128)} %copy-done.1, pred[512,512]{0,1:T(8,128)(4,1)S(1)} %broadcast_compare_fusion), kind=kOutput, calls=%fused_computation.92 | convolution fusion | flops 416414976 | bytes 14445568 | tf_op jit(solution)/shard_map/hqk,qhd->khd/dot_general | solution.py:70
  340.8 9.6 %multiply_reduce_fusion.1 = (f32[12,512]{1,0:T(8,128)S(1)}, f32[12,512,512]{1,2,0:T(8,128)}) fusion(f32[12,512]{1,0:T(8,128)S(1)} %log_add_fusion.1, f32[12,512,512]{1,2,0:T(8,128)} %copy-done.1, pred[512,512]{0,1:T(8,128)(4,1)S(1)} %broadcast_compare_fusion, bf16[512,12,64]{0,2,1:T(8,128)(2,1)S(1)} %bitcast.411, bf16[512,12,64]{0,2,1:T(8,128)(2,1)S(1)} %bitcast.407), kind=kOutput, calls=%fused_computation.4 | convolution fusion | flops 418375680 | bytes 27049984 | tf_op jit(solution)/shard_map/qhd,khd->hqk/dot_general | solution.py:65
  386.6 8.0 fusion.38
  403.7 8.3 convert_reduce_fusion.2
  413.7 11.2 %multiply_reduce_fusion = (f32[12,512]{1,0:T(8,128)S(1)}, f32[12,512,512]{1,2,0:T(8,128)}) fusion(f32[12,512]{1,0:T(8,128)S(1)} %copy-done.63, f32[12,512,512]{1,2,0:T(8,128)} %copy-done, pred[512,512]{0,1:T(8,128)(4,1)S(1)} %broadcast_compare_fusion, bf16[512,12,64]{0,2,1:T(8,128)(2,1)S(1)} %bitcast.409, bf16[512,12,64]{0,2,1:T(8,128)(2,1)S(1)} %bitcast.439), kind=kOutput, calls=%fused_computation.1 | convolution fusion | flops 418375680 | bytes 27049984 | tf_op jit(solution)/shard_map/qhd,khd->hqk/dot_general | solution.py:65
  442.8 7.4 convert_bitcast_fusion
  450.2 8.4 convert_bitcast_fusion.1
  458.6 8.4 pad_maximum_fusion.1
  467.0 12.7 %copy.209 = bf16[8,768,768]{2,1,0:T(8,128)(2,1)} copy(bf16[8,768,768]{1,2,0:T(8,128)(2,1)} %bitcast.378) | data formatting | bytes 18874368 | tf_op jit(solution)/shard_map/reshape | solution.py:294
  480.2 7.3 convert_bitcast_fusion.2
  487.6 7.7 convert_bitcast_fusion.3
  495.3 8.3 pad_maximum_fusion
  503.6 13.4 %copy.205 = bf16[8,768,768]{2,1,0:T(8,128)(2,1)} copy(bf16[8,768,768]{1,2,0:T(8,128)(2,1)} %bitcast.379) | data formatting | bytes 18874368 | tf_op jit(solution)/shard_map/reshape | solution.py:294
  517.1 58.3 %reduce-scatter.11.cloned.1.call-done = bf16[1,768,768]{2,1,0:T(8,128)(2,1)} async-done(((bf16[8,768,768]{2,1,0:T(8,128)(2,1)}), bf16[1,768,768]{2,1,0:T(8,128)(2,1)}) %reduce-scatter.11.cloned.1.call-update) | async-done | bytes 1179664 | tf_op jit(solution)/shard_map/reduce_scatter | solution.py:295
  575.4 80.4 %reduce-scatter.9.cloned.1.call-done = bf16[1,768,768]{2,1,0:T(8,128)(2,1)} async-done(((bf16[8,768,768]{2,1,0:T(8,128)(2,1)}), bf16[1,768,768]{2,1,0:T(8,128)(2,1)}) %reduce-scatter.9.cloned.1.call-update) | async-done | bytes 1179664 | tf_op jit(solution)/shard_map/reduce_scatter | solution.py:295
  657.8 134.5 %all-reduce.3.cloned.1.call-done = (bf16[1,2,192,768]{3,2,1,0:T(8,128)(2,1)}, bf16[1,2,192,768]{3,2,1,0:T(8,128)(2,1)}, bf16[1,768,768]{2,1,0:T(8,128)(2,1)}, bf16[1,768,768]{2,1,0:T(8,128)(2,1)}) async-done(((bf16[1,2,192,768]{3,2,1,0:T(8,128)(2,1)}, bf16[1,2,192,768]{3,2,1,0:T(8,128)(2,1)}, bf16[1,768,768]{2,1,0:T(8,128)(2,1)}, bf16[1,768,768]{2,1,0:T(8,128)(2,1)}), (bf16[1,2,192,768]{3,2,1,0:T(8,128)(2,1)}, ...) | async-done | bytes 3538960 | tf_op jit(solution)/shard_map/psum | solution.py:288
  890.7 10.2 %all-gather.27.cloned.1.call-done = bf16[2,768,768]{2,1,0:T(8,128)(2,1)} async-done(((bf16[1,768,768]{2,1,0:T(8,128)(2,1)}), bf16[2,768,768]{2,1,0:T(8,128)(2,1)}) %all-gather.27.cloned.1.call-update) | async-done | bytes 2359312 | tf_op jit(solution)/shard_map/all_gather | solution.py:297
  (502 shorter events, 293.3 us)
Async XLA Ops:
  7.2 62.2 %all-gather.29.cloned.1.call-start = ((), (), s32[]{:S(2)}) async-start(), calls=%async_computation.22 | async-start | bytes 5308416 | tf_op jit(solution)/shard_map/all_gather | solution.py:185
  10.8 106.8 %all-gather.31.cloned.1.call-start = ((), (), s32[]{:S(2)}) async-start(), calls=%async_computation.23 | async-start | bytes 5308416 | tf_op jit(solution)/shard_map/all_gather | solution.py:185
  11.8 167.0 %all-gather.17.cloned.1.call-start = ((), (), s32[]{:S(2)}) async-start(), calls=%async_computation.12 | async-start | bytes 10616832 | tf_op jit(solution)/shard_map/all_gather | solution.py:196
  16.1 28.2 %all-to-all-start.5 = ((bf16[4,128,768]{2,1,0:T(8,128)(2,1)}), bf16[4,128,768]{2,1,0:T(8,128)(2,1)S(1)}, u32[]{:S(2)}, u32[]{:S(2)}) async-start(bf16[4,128,768]{2,1,0:T(8,128)(2,1)} %bitcast.446), calls=%async_computation.5 | async-start | bytes 1572864 | tf_op jit(solution)/shard_map/all_to_all | solution.py:149
  21.4 273.5 %all-gather.19.cloned.1.call-start = ((), (), s32[]{:S(2)}) async-start(), calls=%async_computation.13 | async-start | bytes 10616832 | tf_op jit(solution)/shard_map/all_gather | solution.py:196
  22.8 166.4 %copy-start.85 = (s32[4]{0:T(128)}, s32[4]{0:T(128)S(1)}, u32[]{:S(2)}) copy-start(s32[4]{0:T(128)S(1)} %bitcast_subtract_fusion) | copy-start | bytes 52
  23.7 267.4 %copy-start.90 = (pred[512]{0:T(512)(128)(4,1)}, pred[512]{0:T(512)(128)(4,1)S(1)}, u32[]{:S(2)}) copy-start(pred[512]{0:T(512)(128)(4,1)S(1)} %broadcast_compare_fusion.1) | copy-start | bytes 1540
  44.3 29.3 %all-to-all-start = ((bf16[4,128,768]{2,1,0:T(8,128)(2,1)}), bf16[4,128,768]{2,1,0:T(8,128)(2,1)S(1)}, u32[]{:S(2)}, u32[]{:S(2)}) async-start(bf16[4,128,768]{2,1,0:T(8,128)(2,1)} %bitcast), calls=%async_computation | async-start | bytes 1572864 | tf_op jit(solution)/shard_map/all_to_all | solution.py:149
  73.5 186.3 %all-to-all-start.2 = ((bf16[4,128,768]{2,1,0:T(8,128)(2,1)}), bf16[4,128,768]{2,1,0:T(8,128)(2,1)}, u32[]{:S(2)}, u32[]{:S(2)}) async-start(bf16[4,128,768]{2,1,0:T(8,128)(2,1)} %bitcast.29), calls=%async_computation.2 | async-start | bytes 1572864 | tf_op jit(solution)/shard_map/all_to_all | solution.py:149
  259.8 122.0 %all-to-all-start.4 = ((bf16[4,128,768]{2,1,0:T(8,128)(2,1)}), bf16[4,128,768]{2,1,0:T(8,128)(2,1)}, u32[]{:S(2)}, u32[]{:S(2)}) async-start(bf16[4,128,768]{2,1,0:T(8,128)(2,1)} %bitcast.54), calls=%async_computation.4 | async-start | bytes 1572864 | tf_op jit(solution)/shard_map/all_to_all | solution.py:149
  264.0 253.0 %reduce-scatter.7.cloned.1.call-start = ((), (), s32[]{:S(2)}) async-start(), calls=%async_computation.16 | async-start | bytes 5308416 | tf_op jit(solution)/shard_map/reduce_scatter | solution.py:287
  375.2 141.9 %reduce-scatter.5.cloned.1.call-start = ((), (), s32[]{:S(2)}) async-start(), calls=%async_computation.14 | async-start | bytes 5308416 | tf_op jit(solution)/shard_map/reduce_scatter | solution.py:287
  442.4 133.0 %reduce-scatter.11.cloned.1.call-start = ((), (), s32[]{:S(2)}) async-start(), calls=%async_computation.20 | async-start | bytes 10616832 | tf_op jit(solution)/shard_map/reduce_scatter | solution.py:295
  479.7 176.1 %reduce-scatter.9.cloned.1.call-start = ((), (), s32[]{:S(2)}) async-start(), calls=%async_computation.18 | async-start | bytes 10616832 | tf_op jit(solution)/shard_map/reduce_scatter | solution.py:295
  517.0 275.3 %all-reduce.3.cloned.1.call-start = ((), (), s32[]{:S(2)}) async-start(), calls=%async_computation.25 | async-start | bytes 7077888 | tf_op jit(solution)/shard_map/psum | solution.py:288
  655.9 214.7 %all-gather.33.cloned.1.call-start = ((), (), s32[]{:S(2)}) async-start(), calls=%async_computation.24 | async-start | bytes 2433024 | tf_op jit(solution)/shard_map/all_gather | solution.py:18
  657.8 219.4 %all-gather.21.cloned.1.call-start = ((), (), s32[]{:S(2)}) async-start(), calls=%async_computation.15 | async-start | bytes 1769472 | tf_op jit(solution)/shard_map/all_gather | solution.py:289
  792.3 86.3 %all-gather.23.cloned.1.call-start = ((), (), s32[]{:S(2)}) async-start(), calls=%async_computation.17 | async-start | bytes 1769472 | tf_op jit(solution)/shard_map/all_gather | solution.py:289
  804.0 15.4 %all-to-all-start.1 = ((bf16[4,2,49152]{2,1,0:T(2,128)(2,1)}), bf16[4,2,49152]{2,1,0:T(2,128)(2,1)}, u32[]{:S(2)}, u32[]{:S(2)}) async-start(bf16[4,2,49152]{2,1,0:T(2,128)(2,1)} %reshape.578), calls=%async_computation.1 | async-start | bytes 1572864 | tf_op jit(solution)/shard_map/all_to_all | solution.py:153
  819.4 18.0 %all-to-all-start.3 = ((bf16[4,2,49152]{2,1,0:T(2,128)(2,1)}), bf16[4,2,49152]{2,1,0:T(2,128)(2,1)}, u32[]{:S(2)}, u32[]{:S(2)}) async-start(bf16[4,2,49152]{2,1,0:T(2,128)(2,1)} %reshape.580), calls=%async_computation.3 | async-start | bytes 1572864 | tf_op jit(solution)/shard_map/all_to_all | solution.py:153
  823.7 63.6 %all-gather.25.cloned.1.call-start = ((), (), s32[]{:S(2)}) async-start(), calls=%async_computation.19 | async-start | bytes 3538944 | tf_op jit(solution)/shard_map/all_gather | solution.py:297
  837.4 15.7 %all-to-all-start.7 = ((bf16[4,2,49152]{2,1,0:T(2,128)(2,1)}), bf16[4,2,49152]{2,1,0:T(2,128)(2,1)S(1)}, u32[]{:S(2)}, u32[]{:S(2)}) async-start(bf16[4,2,49152]{2,1,0:T(2,128)(2,1)} %reshape.584), calls=%async_computation.7 | async-start | bytes 1572864 | tf_op jit(solution)/shard_map/all_to_all | solution.py:153
  853.1 15.8 %all-to-all-start.6 = ((bf16[4,2,49152]{2,1,0:T(2,128)(2,1)}), bf16[4,2,49152]{2,1,0:T(2,128)(2,1)S(1)}, u32[]{:S(2)}, u32[]{:S(2)}) async-start(bf16[4,2,49152]{2,1,0:T(2,128)(2,1)} %reshape.582), calls=%async_computation.6 | async-start | bytes 1572864 | tf_op jit(solution)/shard_map/all_to_all | solution.py:153
  857.3 43.6 %all-gather.27.cloned.1.call-start = ((), (), s32[]{:S(2)}) async-start(), calls=%async_computation.21 | async-start | bytes 3538944 | tf_op jit(solution)/shard_map/all_gather | solution.py:297
  (109 other events, 998.4 us)
Sparse Core Ops, SparseCore 0:
  11.0 58.3 all-gather.28
  71.8 45.8 all-gather.30
  120.1 58.6 all-gather.16
  181.2 60.4 all-gather.18
  375.3 52.3 reduce-scatter.6
  442.5 52.5 reduce-scatter.4
  498.6 76.8 reduce-scatter.10
  578.9 76.8 reduce-scatter.8
  658.4 133.8 all-reduce.2
  795.6 56.2 all-gather.32
  853.4 8.3 all-gather.20
  863.2 10.3 all-gather.22
  875.1 12.1 all-gather.24
  888.7 12.1 all-gather.26
